TPU v7x, 32 devices: a whole 2x2x4 slice. The times are simulated.
32 devices in a mesh: seq: 16 (over z, x, core), ex: 2 (over y).
Axes of the slice: x: 2, y: 2, z: 4, core: 2. Of those that a mesh axis runs over, the one named last changes fastest.
Arguments:
- acts: bfloat16 [4, 2048, 4096], P('ex', 'seq'), may hold values from -6 to 6
- out_grads: bfloat16 [4, 2048, 5120], P('ex', 'seq'), may hold values from -6 to 6
- lengths: int32 [4], P('ex'), may hold values from 512 to 2048, as said below
- in_tiles: bfloat16 [32, 128, 128], replicated, may hold values from -0.09375 to 0.09375
- in_blocks: int32 [32], replicated, may hold values from 0 to 31, each once
- in_signs: int32 [32, 128], replicated, may hold values 0 or 1
- out_tiles: bfloat16 [40, 128, 64], replicated, may hold values from -0.09375 to 0.09375
- out_blocks: int32 [40], replicated, may hold values from 0 to 39, as said below
- out_signs: int32 [40, 128], replicated, may hold values 0 or 1
- query_grads: bfloat16 [2048, 8192], P('seq', 'ex'), may hold values from -6 to 6
Outputs:
- scores: float32 [4, 2048], P('ex', 'seq')
Inputs may be any that keep to these rules, and one draw needn't show every extreme that they name: `lengths`: every training sequence has at least 512 live positions and some sequence has all 2048. `in_blocks`: a permutation of the 32 input feature blocks. `out_blocks`: the first 32 entries are a permutation of 0 to 31, the last 8 a permutation of 32 to 39.
All inputs are finite; a program needn't handle non-finite values.
Results may differ from a plain program's by a relative error of at most 0.005.
Values may be sent and summed in bfloat16 or wider, within the bound.
A program may use at most 64 MiB of HBM per device.

v0:
```python
import jax
import jax.numpy as jnp
from jax import lax
from jax.sharding import PartitionSpec as P


def place(sketch_tiles, block_ids, sign_bits):
    tile_count = sketch_tiles.shape[0]
    chosen = (block_ids[:, None] == jnp.arange(tile_count, dtype=jnp.int32)[None, :]).astype(
        jnp.float32
    )
    signed = sketch_tiles.astype(jnp.float32) * (2 * sign_bits - 1).astype(jnp.float32)[:, :, None]
    placed = jnp.einsum("bc,bik->cik", chosen, signed, precision=lax.Precision.HIGHEST)
    return placed.reshape(tile_count * sketch_tiles.shape[1], sketch_tiles.shape[2]).astype(
        jnp.bfloat16
    )


def widen(placed, split_at):
    out_cols = placed.shape[1]
    upper = jnp.concatenate([placed[:split_at], jnp.zeros((split_at, out_cols), jnp.bfloat16)], 1)
    lower = jnp.concatenate(
        [jnp.zeros((placed.shape[0] - split_at, out_cols), jnp.bfloat16), placed[split_at:]], 1
    )
    return jnp.concatenate([upper, lower], 0)


def per_device(
    acts,
    out_grads,
    lengths,
    in_tiles,
    in_blocks,
    in_signs,
    out_tiles,
    out_blocks,
    out_signs,
    query_grads,
):
    examples_dev, seq_dev, width = acts.shape
    r_in = place(in_tiles, in_blocks, in_signs)
    r_out = widen(place(out_tiles, out_blocks, out_signs), width)
    offset = lax.axis_index("seq") * seq_dev
    positions = offset + jnp.arange(seq_dev, dtype=jnp.int32)
    live_rows = (positions[None, :] < lengths[:, None]).astype(jnp.float32)
    in_sketched = jnp.dot(
        acts.reshape(examples_dev * seq_dev, width), r_in, preferred_element_type=jnp.float32
    )
    in_sketched = (in_sketched.reshape(examples_dev, seq_dev, -1) * live_rows[:, :, None]).astype(
        jnp.bfloat16
    )
    out_sketched = jnp.dot(
        out_grads.reshape(examples_dev * seq_dev, -1), r_out, preferred_element_type=jnp.float32
    )
    out_sketched = out_sketched.reshape(examples_dev, seq_dev, -1).astype(jnp.bfloat16)
    crossed = jnp.einsum(
        "esa,esc->eac", in_sketched, out_sketched, preferred_element_type=jnp.float32
    )
    in_cols = r_in.shape[1] // 2
    out_cols = r_out.shape[1] // 2
    partial_proj = jnp.stack([crossed[:, :in_cols, :out_cols], crossed[:, in_cols:, out_cols:]], 1)
    partial_proj = partial_proj.reshape(examples_dev, -1) / lengths.astype(jnp.float32)[:, None]
    proj_width = partial_proj.shape[1]
    ex_count = lax.axis_size("ex")
    block_width = proj_width // ex_count
    pieces = partial_proj.reshape(examples_dev, ex_count, block_width)
    moved = lax.all_to_all(pieces, "ex", split_axis=1, concat_axis=0, tiled=True)
    summed = lax.psum(moved, "seq")
    owned = summed.astype(jnp.bfloat16).reshape(examples_dev * ex_count, block_width)
    return lax.psum_scatter(
        lax.dot_general(
            owned, query_grads, (((1,), (1,)), ((), ())), preferred_element_type=jnp.float32
        ),
        "ex",
        scatter_dimension=0,
        tiled=True,
    )


def solution(mesh):
    in_specs = (
        P("ex", "seq", None),
        P("ex", "seq", None),
        P("ex"),
        P(),
        P(),
        P(),
        P(),
        P(),
        P(),
        P("seq", "ex"),
    )
    out_specs = P("ex", "seq")
    return jax.shard_map(
        per_device, mesh=mesh, in_specs=in_specs, out_specs=out_specs, check_vma=False
    )
```

profile of v0, /device:TPU:0, one launch (start us, length us, event | category | flops | bytes accessed | tf_op | source)
XLA Modules:
  0.0 92.1 jit_solution(9811729410962465294)
XLA Ops:
  0.0 0.9 add_convert_fusion
  0.9 1.2 %convert_multiply_fusion.1 = f32[40,128,64]{1,2,0:T(8,128)S(1)} fusion(bf16[40,128,64]{1,2,0:T(8,128)(2,1)} %param.16, f32[40,128]{1,0:T(8,128)S(1)} %add_convert_fusion), kind=kLoop, calls=%fused_computation.15 | loop fusion | flops 655360 | bytes 1986560 | tf_op jit(solution)/shard_map/mul | solution.py:12
  2.1 2.3 %convolution_convert_fusion = bf16[40,128,64]{1,0,2:T(8,128)(2,1)S(1)} fusion(f32[40,128,64]{1,2,0:T(8,128)S(1)} %convert_multiply_fusion.1, s32[40]{0:T(128)} %param.17), kind=kOutput, calls=%fused_computation.8 | convolution fusion | flops 157615680 | bytes 1966240 | tf_op jit(solution)/shard_map/bc,bik->cik/dot_general | solution.py:13
  4.5 0.2 copy.39
  4.8 1.0 %fusion.18 = bf16[256,128]{0,1:T(8,128)(2,1)S(1)} fusion(bf16[256,5120]{1,0:T(8,128)(2,1)S(1)} %bitcast.46, bf16[1024,64]{0,1:T(8,128)(2,1)S(1)} %bitcast.54, bf16[4096,64]{0,1:T(8,128)(2,1)S(1)} %bitcast.50), kind=kOutput, calls=%fused_computation.18 | convolution fusion | flops 340819968 | bytes 3342336 | tf_op jit(solution)/shard_map/dot_general | solution.py:52
  5.8 0.1 copy.25
  5.9 1.8 %convert_multiply_fusion = f32[32,128,128]{2,1,0:T(8,128)S(1)} fusion(bf16[32,128,128]{2,1,0:T(8,128)(2,1)} %param.13, f32[32,128]{1,0:T(8,128)S(1)} %add_convert_fusion.1), kind=kLoop, calls=%fused_computation.6 | loop fusion | flops 1048576 | bytes 3162112 | tf_op jit(solution)/shard_map/mul | solution.py:12
  7.8 2.4 %fusion.4 = bf16[32,128,128]{2,0,1:T(8,128)(2,1)S(1)} fusion(f32[32,128,128]{2,1,0:T(8,128)S(1)} %convert_multiply_fusion, s32[32]{0:T(128)S(1)} %copy-done.3), kind=kOutput, calls=%fused_computation.7 | convolution fusion | flops 201851904 | bytes 3145856 | tf_op jit(solution)/shard_map/bc,bik->cik/dot_general | solution.py:13
  10.2 1.4 %copy.21 = bf16[32,128,128]{2,1,0:T(8,128)(2,1)} copy(bf16[32,128,128]{2,0,1:T(8,128)(2,1)S(1)} %fusion.4) | data formatting | bytes 2097152 | tf_op jit(solution)/shard_map/convert_element_type | solution.py:14
  11.6 0.1 compare_convert_fusion
  11.7 2.7 %convolution_bitcast_fusion = f32[16,2,8,128]{3,2,1,0:T(8,128)S(1)} fusion(bf16[4096,128]{1,0:T(8,128)(2,1)} %bitcast.47, bf16[256,4096]{1,0:T(8,128)(2,1)} %bitcast.48), kind=kOutput, calls=%fused_computation.16 | convolution fusion | flops 268435456 | bytes 3276800 | tf_op jit(solution)/shard_map/dot_general | solution.py:46
  14.4 0.1 fusion.23
  14.6 0.1 fusion.38
  14.7 0.1 stack.10
  14.8 0.1 stack.9
  14.9 0.7 maximum_divide_fusion
  15.6 4.3 %all-to-all-start = ((f32[2,2,4096]{2,0,1:T(2,128)}), f32[2,2,4096]{2,0,1:T(2,128)S(1)}, u32[]{:S(2)}, u32[]{:S(2)}) async-start(f32[2,2,4096]{2,0,1:T(2,128)} %maximum_divide_fusion), calls=%async_computation | async-start | bytes 131072 | tf_op jit(solution)/shard_map/all_to_all | solution.py:67
  19.9 0.6 dynamic-slice
  21.1 2.9 %all-to-all-done = f32[2,2,4096]{2,0,1:T(2,128)S(1)} async-done(((f32[2,2,4096]{2,0,1:T(2,128)}), f32[2,2,4096]{2,0,1:T(2,128)S(1)}, u32[]{:S(2)}, u32[]{:S(2)}) %all-to-all-start) | async-done | bytes 65568 | tf_op jit(solution)/shard_map/all_to_all | solution.py:67
  24.0 0.1 all_to_all.16
  24.0 60.9 %psum.7 = bf16[4,1,4096]{2,0,1:T(4,128)(2,1)S(1)} all-reduce(f32[4,1,4096]{2,0,1:T(4,128)S(1)} %all_to_all.16), channel_id=1, replica_groups=mesh['seq'=16,'ex'=2] {'seq'}, use_global_device_ids=true, to_apply=%region_0.0 | all-reduce | flops 16384 | bytes 98304 | tf_op jit(solution)/shard_map/psum | solution.py:68
  85.0 1.6 %fusion.26 = f32[4,128]{1,0:T(4,128)S(1)} fusion(bf16[128,4096]{1,0:T(8,128)(2,1)} %param.19, bf16[4,1,4096]{2,0,1:T(4,128)(2,1)S(1)} %psum.7), kind=kOutput, calls=%fused_computation.27 | convolution fusion | flops 4194304 | bytes 1083392 | tf_op jit(solution)/shard_map/dot_general | solution.py:71
  86.6 4.9 %all-reduce.2 = f32[4,128]{1,0:T(4,128)S(1)} all-reduce(f32[4,128]{1,0:T(4,128)S(1)} %fusion.26), channel_id=2, replica_groups=mesh['seq'=16,'ex'=2] {'ex'}, use_global_device_ids=true, to_apply=%region_1.0.clone | all-reduce | flops 512 | bytes 4096
  91.5 0.6 constant_dynamic-slice_fusion
  (16 shorter events, 0.1 us)
Async XLA Ops:
  0.0 4.7 %copy-start = (bf16[2,128,5120]{2,1,0:T(8,128)(2,1)S(1)}, bf16[2,128,5120]{2,1,0:T(8,128)(2,1)}, u32[]{:S(2)}) copy-start(bf16[2,128,5120]{2,1,0:T(8,128)(2,1)} %param.11) | copy-start | bytes 7864324
  4.7 1.1 %copy-start.1 = (s32[32,128]{1,0:T(8,128)S(1)}, s32[32,128]{1,0:T(8,128)}, u32[]{:S(2)}) copy-start(s32[32,128]{1,0:T(8,128)} %param.15) | copy-start | bytes 49156
  5.8 2.0 %copy-start.3 = (s32[32]{0:T(128)S(1)}, s32[32]{0:T(128)}, u32[]{:S(2)}) copy-start(s32[32]{0:T(128)} %param.14) | copy-start | bytes 388
  7.8 3.9 %copy-start.2 = (s32[2]{0:T(128)S(1)}, s32[2]{0:T(128)}, u32[]{:S(2)}) copy-start(s32[2]{0:T(128)} %param.12) | copy-start | bytes 28
  11.7 8.2 %copy-start.4 = (u32[32]{0:T(128)S(1)}, u32[32]{0:T(128)}, u32[]{:S(2)}) copy-start(u32[32]{0:T(128)} %constant.25) | copy-start | bytes 388
  15.6 8.4 %all-to-all-start = ((f32[2,2,4096]{2,0,1:T(2,128)}), f32[2,2,4096]{2,0,1:T(2,128)S(1)}, u32[]{:S(2)}, u32[]{:S(2)}) async-start(f32[2,2,4096]{2,0,1:T(2,128)} %maximum_divide_fusion), calls=%async_computation | async-start | bytes 131072 | tf_op jit(solution)/shard_map/all_to_all | solution.py:67
where the time goes:
time: 92.4 us; the launch traced here: 92.1 us
  blocking collectives  65.9 us (71%)
  matrix products  10.2 us (11%)
  other arithmetic  4.75 us (5%)
  starting transfers between devices  4.26 us (5%)
  local copies, waits for them, and re-layouts  3.29 us (4%)
  waiting for transfers between devices  2.89 us (3%)
    psum x1, blocking collectives, per_device(): summed = lax.psum(moved, 'seq')  60.9 us
    unnamed x1, blocking collectives  4.93 us
    dot_general x2, matrix products, place(): jnp.einsum('bc,bik->cik', chosen, signed, precision=lax.Precision.HIGHEST)  4.72 us
    all_to_all x1, starting transfers between devices, per_device(): lax.all_to_all(pieces, 'ex', split_axis=1, concat_axis=0, tiled=True)  4.26 us
    mul x2, other arithmetic, place(): sketch_tiles.astype(jnp.float32)  3.08 us
    all_to_all x1, waiting for transfers between devices, per_device(): lax.all_to_all(pieces, 'ex', split_axis=1, concat_axis=0, tiled=True)  2.89 us
    dot_general x1, matrix products, per_device(): jnp.dot(acts.reshape(examples_dev * seq_dev, width), r_in, preferred_elem...  2.74 us
  transfers between devices with their start and end apart: 1, of which 1 were waited for; matrix products, arithmetic and copies ran while one was open for 1% of the time, Pallas kernels for 0%

commit v1 on v0

v1 whole, which is shorter than its diff:
```python
import functools

import jax
import jax.numpy as jnp
from jax import lax
from jax.experimental import pallas as pl
from jax.experimental.pallas import tpu as pltpu
from jax.sharding import PartitionSpec as P

MESH = pl.DeviceIdType.MESH
SUBLANES = 16


def signed_columns(rows_ref, blocks_ref, signs_ref, first, count):
    _, examples, positions, width = rows_ref.shape
    signs = (2 * signs_ref[...] - 1).astype(jnp.float32).astype(jnp.bfloat16)
    columns = []
    for b in range(first, first + count):
        block = rows_ref[blocks_ref[b]].reshape(examples * positions, width)
        columns.append(block * signs[b : b + 1, :])
    return jnp.concatenate(columns, axis=1)


def body(
    seq_count,
    ex_count,
    inner,
    lengths_ref,
    in_blocks_ref,
    out_blocks_ref,
    acts_hbm,
    grads_hbm,
    in_tiles_hbm,
    in_signs_hbm,
    out_tiles_hbm,
    out_signs_hbm,
    query_hbm,
    out_ref,
    acts,
    grads,
    in_tiles,
    in_signs,
    out_tiles,
    out_signs,
    query,
    pieces,
    a_recv,
    b_send,
    b_recv,
    ordered,
    c_send,
    c_recv,
    d_send,
    d_recv,
    load_sem,
    a_ssem,
    a_rsem,
    b_ssem,
    b_rsem,
    c_ssem,
    c_rsem,
    d_ssem,
    d_rsem,
):
    outer = seq_count // inner
    s = lax.axis_index("seq")
    x = lax.axis_index("ex")
    o = s // inner
    i = lax.rem(s, inner)

    loads = {}
    for n, (name, src, dst) in enumerate(
        (
            ("in_signs", in_signs_hbm, in_signs),
            ("out_signs", out_signs_hbm, out_signs),
            ("in_tiles", in_tiles_hbm, in_tiles),
            ("acts", acts_hbm, acts),
            ("out_tiles", out_tiles_hbm, out_tiles),
            ("grads", grads_hbm, grads),
            ("query", query_hbm, query),
        )
    ):
        if src.shape == dst.shape:
            loads[name] = pltpu.make_async_copy(src, dst, load_sem.at[n])
            loads[name].start()
            continue
        width = dst.shape[3]
        for b in range(dst.shape[0]):
            pltpu.make_async_copy(
                src.at[:, :, b * width : (b + 1) * width], dst.at[b], load_sem.at[n]
            ).start()
        loads[name] = pltpu.make_async_copy(dst, dst, load_sem.at[n])

    def at(outer_step, inner_step, ex_step):
        to_o = lax.rem(o + outer_step, outer)
        to_i = lax.rem(i + inner_step, inner)
        to_x = lax.rem(x + ex_step, ex_count)
        return to_o * inner + to_i, to_x

    near = [(di, dx) for dx in range(ex_count) for di in range(inner) if di or dx]
    barrier = pltpu.get_barrier_semaphore()
    peers = [(0, di, dx) for di, dx in near] + [(do, 0, 0) for do in range(1, outer)]
    for steps in peers:
        to_s, to_x = at(*steps)
        pl.semaphore_signal(barrier, 1, device_id=(to_s, to_x), device_id_type=MESH)

    _, examples, positions, _ = acts.shape
    in_count = in_tiles.shape[0]
    out_count = out_tiles.shape[0]
    cols = out_tiles.shape[1]
    f32 = jnp.float32

    loads["in_signs"].wait()
    loads["in_tiles"].wait()
    loads["acts"].wait()
    left = signed_columns(acts, in_blocks_ref, in_signs, 0, in_count)
    tiles = in_tiles[...].reshape(-1, in_tiles.shape[2])
    in_sketched = jnp.dot(left, tiles, preferred_element_type=f32)
    place = s * positions + lax.broadcasted_iota(jnp.int32, (positions, 1), 0)
    in_parts = [
        jnp.where(
            place < lengths_ref[e], in_sketched[e * positions : (e + 1) * positions], 0.0
        ).astype(jnp.bfloat16)
        for e in range(examples)
    ]

    loads["out_signs"].wait()
    loads["out_tiles"].wait()
    loads["grads"].wait()
    upper = signed_columns(grads, out_blocks_ref, out_signs, 0, in_count)
    lower = signed_columns(grads, out_blocks_ref, out_signs, in_count, out_count - in_count)
    halves = [
        lax.dot_general(
            left,
            jnp.concatenate([out_tiles[b] for b in range(first, last)], axis=1),
            (((1,), (1,)), ((), ())),
            preferred_element_type=f32,
        ).astype(jnp.bfloat16)
        for left, first, last in ((upper, 0, in_count), (lower, in_count, out_count))
    ]

    half_rows = in_parts[0].shape[1] // 2
    piece_rows = pieces.shape[1]
    crossed = [[], []]
    for e in range(examples):
        out_part = jnp.concatenate(
            [half[e * positions : (e + 1) * positions] for half in halves], axis=1
        )
        full = lax.dot_general(
            in_parts[e], out_part, (((0,), (0,)), ((), ())), preferred_element_type=f32
        )
        full = full / lengths_ref[e].astype(f32)
        crossed[0].append(full[:half_rows, :cols])
        crossed[1].append(full[half_rows:, cols:])
    joined = jnp.concatenate([jnp.concatenate(part, axis=1) for part in crossed], axis=0)
    for p in range(pieces.shape[0]):
        pieces[p] = joined[p * piece_rows : (p + 1) * piece_rows]

    pl.semaphore_wait(barrier, len(peers))

    sends = []

    def push(src, dst, ssem, rsem, steps):
        to_s, to_x = at(*steps)
        copy = pltpu.make_async_remote_copy(
            src, dst, ssem, rsem, device_id=(to_s, to_x), device_id_type=MESH
        )
        copy.start()
        sends.append(copy)
        return copy

    got = {}
    for di, dx in near:
        to_i = lax.rem(i + di, inner)
        to_x = lax.rem(x + dx, ex_count)
        slot = dx * inner + di
        got[slot] = push(
            pieces.at[to_x * inner + to_i],
            a_recv.at[slot],
            a_ssem.at[slot],
            a_rsem.at[slot],
            (0, di, dx),
        )
    own = pieces[x * inner + i]
    for dx in range(ex_count):
        total = own if dx == 0 else None
        for di in range(inner):
            slot = dx * inner + di
            if slot == 0:
                continue
            got[slot].wait_recv()
            total = a_recv[slot] if total is None else total + a_recv[slot]
        b_send[dx] = total

    arrivals = [
        push(b_send, b_recv.at[do], b_ssem.at[do], b_rsem.at[do], (do, 0, 0))
        for do in range(1, outer)
    ]
    summed = b_send[...]
    for do, copy in enumerate(arrivals, 1):
        copy.wait_recv()
        summed = summed + b_recv[do]
    b_recv[0] = summed

    all_examples = ex_count * examples
    pairs = piece_rows // 2
    for dx in range(ex_count):
        even = b_recv[0, dx, pl.ds(0, pairs, stride=2), :]
        odd = b_recv[0, dx, pl.ds(1, pairs, stride=2), :]
        for e in range(examples):
            lanes = slice(e * cols, (e + 1) * cols)
            ordered[pl.ds(dx * examples + e, pairs, stride=all_examples), :] = jnp.concatenate(
                [even[:, lanes], odd[:, lanes]], axis=1
            )
    c_send[...] = ordered[...].astype(jnp.bfloat16)
    arrivals = [
        push(c_send, c_recv.at[di], c_ssem.at[di], c_rsem.at[di], (0, di, 0))
        for di in range(1, inner)
    ]

    loads["query"].wait()
    width = 2 * cols
    group = max(SUBLANES, all_examples)
    per_group = group // all_examples
    groups = c_send.shape[0] // group
    sums = [None] * per_group
    for di in range(inner):
        if di:
            arrivals[di - 1].wait_recv()
        from_i = lax.rem(i - di + inner, inner)
        chunk = c_recv[di] if di else c_send[...]
        left = jnp.concatenate(
            [chunk[u * group : (u + 1) * group] for u in range(groups)], axis=1
        )
        for j in range(per_group):
            right = jnp.concatenate(
                [
                    query[
                        :,
                        pl.ds(
                            pl.multiple_of((from_i * pairs + u * per_group + j) * width, width),
                            width,
                        ),
                    ]
                    for u in range(groups)
                ],
                axis=1,
            )
            term = lax.dot_general(
                left, right, (((1,), (1,)), ((), ())), preferred_element_type=f32
            )
            sums[j] = term if sums[j] is None else sums[j] + term
    scores = sums[0][:all_examples]
    for j in range(1, per_group):
        scores = scores + sums[j][j * all_examples : (j + 1) * all_examples]

    for dx in range(1, ex_count):
        d_send[dx] = scores[dx * examples : (dx + 1) * examples]
    arrivals = [
        push(
            d_send.at[dx], d_recv.at[dx], d_ssem.at[dx], d_rsem.at[dx], (0, 0, ex_count - dx)
        )
        for dx in range(1, ex_count)
    ]
    result = scores[:examples]
    for dx, copy in enumerate(arrivals, 1):
        copy.wait_recv()
        result = result + d_recv[dx]
    out_ref[...] = result
    for copy in sends:
        copy.wait_send()


def per_device(
    seq_count,
    ex_count,
    acts,
    out_grads,
    lengths,
    in_tiles,
    in_blocks,
    in_signs,
    out_tiles,
    out_blocks,
    out_signs,
    query_grads,
):
    examples = acts.shape[0]
    queries = query_grads.shape[0]
    in_cols = in_tiles.shape[2]
    cols = out_tiles.shape[2]
    inner = 4 if seq_count % 4 == 0 else 1
    outer = seq_count // inner
    piece_rows = in_cols // (ex_count * inner)
    lanes = examples * cols
    gathered = piece_rows // 2 * ex_count * examples
    smem = pl.BlockSpec(memory_space=pltpu.SMEM)
    hbm = pl.BlockSpec(memory_space=pl.ANY)
    f32 = jnp.float32
    out_tiles = jnp.swapaxes(out_tiles, 1, 2)
    arrays = (acts, out_grads, in_tiles, in_signs, out_tiles, out_signs, query_grads)
    tile = in_tiles.shape[1]
    shapes = [a.shape for a in arrays]
    shapes[0] = (in_tiles.shape[0],) + acts.shape[:2] + (tile,)
    shapes[1] = (out_tiles.shape[0],) + acts.shape[:2] + (tile,)
    slots = ex_count * inner
    return pl.pallas_call(
        functools.partial(body, seq_count, ex_count, inner),
        out_shape=jax.ShapeDtypeStruct((examples, queries), f32),
        in_specs=[smem] * 3 + [hbm] * 7,
        out_specs=pl.BlockSpec(memory_space=pltpu.VMEM),
        scratch_shapes=[pltpu.VMEM(shape, a.dtype) for shape, a in zip(shapes, arrays)]
        + [
            pltpu.VMEM((slots, piece_rows, lanes), f32),
            pltpu.VMEM((slots, piece_rows, lanes), f32),
            pltpu.VMEM((ex_count, piece_rows, lanes), f32),
            pltpu.VMEM((outer, ex_count, piece_rows, lanes), f32),
            pltpu.VMEM((gathered, lanes), f32),
            pltpu.VMEM((gathered, lanes), jnp.bfloat16),
            pltpu.VMEM((inner, gathered, lanes), jnp.bfloat16),
            pltpu.VMEM((ex_count, examples, queries), f32),
            pltpu.VMEM((ex_count, examples, queries), f32),
            pltpu.SemaphoreType.DMA((len(arrays),)),
            pltpu.SemaphoreType.DMA((slots,)),
            pltpu.SemaphoreType.DMA((slots,)),
            pltpu.SemaphoreType.DMA((outer,)),
            pltpu.SemaphoreType.DMA((outer,)),
            pltpu.SemaphoreType.DMA((inner,)),
            pltpu.SemaphoreType.DMA((inner,)),
            pltpu.SemaphoreType.DMA((ex_count,)),
            pltpu.SemaphoreType.DMA((ex_count,)),
        ],
        compiler_params=pltpu.CompilerParams(collective_id=0, has_side_effects=True),
        name="scores",
    )(lengths, in_blocks, out_blocks, *arrays)


def solution(mesh):
    in_specs = (
        P("ex", "seq", None),
        P("ex", "seq", None),
        P("ex"),
        P(),
        P(),
        P(),
        P(),
        P(),
        P(),
        P("seq", "ex"),
    )
    return jax.shard_map(
        functools.partial(per_device, mesh.shape["seq"], mesh.shape["ex"]),
        mesh=mesh,
        in_specs=in_specs,
        out_specs=P("ex", "seq"),
        check_vma=False,
    )
```

time: 92.4 us -> 23.3 us (0.25)
  blocking collectives: 65.9 us -> 0 us
  Pallas kernels: 0 us -> 21.8 us
  matrix products: 10.2 us -> 0 us
  other arithmetic: 4.75 us -> 0 us
  starting transfers between devices: 4.26 us -> 0 us
  waiting for transfers between devices: 2.89 us -> 0 us
  local copies, waits for them, and re-layouts: 3.29 us -> 1.24 us
    psum x1 -> x0, blocking collectives: 60.9 us -> none  [per_device(): summed = lax.psum(moved, 'seq')]
    pallas_call x0 -> x1, Pallas kernels: none -> 21.8 us  [per_device(): pl.pallas_call(functools.partial(body, seq_count, ex_count, inner), out_s...]
    dot_general x6 -> x0, matrix products: 10.2 us -> none  [the longest x2 4.72 us: place(): jnp.einsum('bc,bik->cik', chosen, signed, precision=lax.Precision.HIGHEST)]
    unnamed x1 -> x0, blocking collectives: 4.93 us -> none
    all_to_all x1 -> x0, starting transfers between devices: 4.26 us -> none  [per_device(): lax.all_to_all(pieces, 'ex', split_axis=1, concat_axis=0, tiled=True)]
    mul x2 -> x0, other arithmetic: 3.08 us -> none  [place(): sketch_tiles.astype(jnp.float32)]
    all_to_all x1 -> x0, waiting for transfers between devices: 2.89 us -> none  [per_device(): lax.all_to_all(pieces, 'ex', split_axis=1, concat_axis=0, tiled=True)]
    convert_element_type x2 -> x0, local copies, waits for them, and re-layouts: 1.49 us -> none  [the longest x1 1.38 us: place(): placed.reshape(tile_count * sketch_tiles.shape[1], sketch_tiles.shape[2])]
  transfers between devices with their start and end apart: 1 -> 0, of which waited for: 1 -> 0; matrix products, arithmetic and copies ran while one was open for 1% -> 0% of each run, Pallas kernels for 0% -> 0%
where the time goes in v1:
time: 23.3 us; the launch traced here: 23 us
  Pallas kernels  21.8 us (94%)
  local copies, waits for them, and re-layouts  1.24 us (5%)
    pallas_call x1, Pallas kernels, per_device(): pl.pallas_call(functools.partial(body, seq_count, ex_count, inner), out_s...  21.8 us
    unnamed x1, local copies, waits for them, and re-layouts  1.24 us

profile of v1, /device:TPU:0, one launch (start us, length us, event | category | flops | bytes accessed | tf_op | source)
XLA Modules:
  0.0 23.0 jit_solution(2011911971153800536)
XLA Ops:
  0.0 21.8 %scores.1 = f32[2,128]{1,0:T(2,128)} custom-call(s32[2]{0:T(128)} %lengths_ref.1, s32[32]{0:T(128)} %in_blocks_ref.1, s32[40]{0:T(128)} %out_blocks_ref.1, bf16[2,128,4096]{2,1,0:T(8,128)(2,1)} %acts_hbm.1, bf16[2,128,5120]{2,1,0:T(8,128)(2,1)} %grads_hbm.1, bf16[32,128,128]{2,1,0:T(8,128)(2,1)} %in_tiles_hbm.1, s32[32,128]{1,0:T(8,128)} %in_signs_hbm.1, ...), custom_call_target="tpu_custom_call" | custom-call | tf_op jit(solution)/shard_map/scores/pallas_call | solution.py:307
  21.8 1.2 %copy.12 = f32[2,128]{1,0:T(2,128)} copy(f32[2,128]{1,0:T(2,128)} %scores.1) | data formatting | bytes 2048

commit v2 on v1

--- a/solution.py
+++ b/solution.py
@@ -12,12 +12,10 @@
 
 
 def signed_columns(rows_ref, blocks_ref, signs_ref, first, count):
-    _, examples, positions, width = rows_ref.shape
     signs = (2 * signs_ref[...] - 1).astype(jnp.float32).astype(jnp.bfloat16)
     columns = []
     for b in range(first, first + count):
-        block = rows_ref[blocks_ref[b]].reshape(examples * positions, width)
-        columns.append(block * signs[b : b + 1, :])
+        columns.append(rows_ref[blocks_ref[b]] * signs[b : b + 1, :])
     return jnp.concatenate(columns, axis=1)
 
 
@@ -69,27 +67,27 @@
     i = lax.rem(s, inner)
 
     loads = {}
-    for n, (name, src, dst) in enumerate(
-        (
-            ("in_signs", in_signs_hbm, in_signs),
-            ("out_signs", out_signs_hbm, out_signs),
-            ("in_tiles", in_tiles_hbm, in_tiles),
-            ("acts", acts_hbm, acts),
-            ("out_tiles", out_tiles_hbm, out_tiles),
-            ("grads", grads_hbm, grads),
-            ("query", query_hbm, query),
-        )
+    examples = len(acts)
+    positions = acts[0].shape[1]
+    for n, name, src, dst in (
+        (0, "in_signs", in_signs_hbm, in_signs),
+        (1, "out_signs", out_signs_hbm, out_signs),
+        (2, "in_tiles", in_tiles_hbm, in_tiles),
+        (5, "acts", acts_hbm, acts),
+        (3, "out_tiles", out_tiles_hbm, out_tiles),
+        (5 + examples, "grads", grads_hbm, grads),
     ):
-        if src.shape == dst.shape:
+        if not isinstance(dst, tuple):
             loads[name] = pltpu.make_async_copy(src, dst, load_sem.at[n])
             loads[name].start()
             continue
-        width = dst.shape[3]
-        for b in range(dst.shape[0]):
-            pltpu.make_async_copy(
-                src.at[:, :, b * width : (b + 1) * width], dst.at[b], load_sem.at[n]
-            ).start()
-        loads[name] = pltpu.make_async_copy(dst, dst, load_sem.at[n])
+        for e, part in enumerate(dst):
+            width = part.shape[2]
+            for b in range(part.shape[0]):
+                pltpu.make_async_copy(
+                    src.at[e, :, b * width : (b + 1) * width], part.at[b], load_sem.at[n + e]
+                ).start()
+            loads[name, e] = pltpu.make_async_copy(part, part, load_sem.at[n + e])
 
     def at(outer_step, inner_step, ex_step):
         to_o = lax.rem(o + outer_step, outer)
@@ -104,7 +102,6 @@
         to_s, to_x = at(*steps)
         pl.semaphore_signal(barrier, 1, device_id=(to_s, to_x), device_id_type=MESH)
 
-    _, examples, positions, _ = acts.shape
     in_count = in_tiles.shape[0]
     out_count = out_tiles.shape[0]
     cols = out_tiles.shape[1]
@@ -112,39 +109,44 @@
 
     loads["in_signs"].wait()
     loads["in_tiles"].wait()
-    loads["acts"].wait()
-    left = signed_columns(acts, in_blocks_ref, in_signs, 0, in_count)
     tiles = in_tiles[...].reshape(-1, in_tiles.shape[2])
-    in_sketched = jnp.dot(left, tiles, preferred_element_type=f32)
     place = s * positions + lax.broadcasted_iota(jnp.int32, (positions, 1), 0)
-    in_parts = [
-        jnp.where(
-            place < lengths_ref[e], in_sketched[e * positions : (e + 1) * positions], 0.0
-        ).astype(jnp.bfloat16)
-        for e in range(examples)
-    ]
+    in_parts = []
+    for e in range(examples):
+        loads["acts", e].wait()
+        left = signed_columns(acts[e], in_blocks_ref, in_signs, 0, in_count)
+        in_sketched = jnp.dot(left, tiles, preferred_element_type=f32)
+        in_parts.append(
+            jnp.where(place < lengths_ref[e], in_sketched, 0.0).astype(jnp.bfloat16)
+        )
 
     loads["out_signs"].wait()
     loads["out_tiles"].wait()
-    loads["grads"].wait()
-    upper = signed_columns(grads, out_blocks_ref, out_signs, 0, in_count)
-    lower = signed_columns(grads, out_blocks_ref, out_signs, in_count, out_count - in_count)
-    halves = [
-        lax.dot_general(
-            left,
-            jnp.concatenate([out_tiles[b] for b in range(first, last)], axis=1),
-            (((1,), (1,)), ((), ())),
-            preferred_element_type=f32,
-        ).astype(jnp.bfloat16)
-        for left, first, last in ((upper, 0, in_count), (lower, in_count, out_count))
+    spans = ((0, in_count), (in_count, out_count))
+    half_tiles = [
+        jnp.concatenate([out_tiles[b] for b in range(first, last)], axis=1)
+        for first, last in spans
     ]
 
     half_rows = in_parts[0].shape[1] // 2
     piece_rows = pieces.shape[1]
     crossed = [[], []]
     for e in range(examples):
+        loads["grads", e].wait()
+        if e == examples - 1:
+            loads["query"] = pltpu.make_async_copy(query_hbm, query, load_sem.at[4])
+            loads["query"].start()
         out_part = jnp.concatenate(
-            [half[e * positions : (e + 1) * positions] for half in halves], axis=1
+            [
+                lax.dot_general(
+                    signed_columns(grads[e], out_blocks_ref, out_signs, first, last - first),
+                    right,
+                    (((1,), (1,)), ((), ())),
+                    preferred_element_type=f32,
+                ).astype(jnp.bfloat16)
+                for right, (first, last) in zip(half_tiles, spans)
+            ],
+            axis=1,
         )
         full = lax.dot_general(
             in_parts[e], out_part, (((0,), (0,)), ((), ())), preferred_element_type=f32
@@ -300,16 +302,17 @@
     out_tiles = jnp.swapaxes(out_tiles, 1, 2)
     arrays = (acts, out_grads, in_tiles, in_signs, out_tiles, out_signs, query_grads)
     tile = in_tiles.shape[1]
-    shapes = [a.shape for a in arrays]
-    shapes[0] = (in_tiles.shape[0],) + acts.shape[:2] + (tile,)
-    shapes[1] = (out_tiles.shape[0],) + acts.shape[:2] + (tile,)
+    held = [pltpu.VMEM(a.shape, a.dtype) for a in arrays]
+    for n, tiles in ((0, in_tiles), (1, out_tiles)):
+        part = pltpu.VMEM((tiles.shape[0], acts.shape[1], tile), arrays[n].dtype)
+        held[n] = (part,) * examples
     slots = ex_count * inner
     return pl.pallas_call(
         functools.partial(body, seq_count, ex_count, inner),
-        out_shape=jax.ShapeDtypeStruct((examples, queries), f32),
+        out_shape=pltpu.VMEM((examples, queries), f32),
         in_specs=[smem] * 3 + [hbm] * 7,
         out_specs=pl.BlockSpec(memory_space=pltpu.VMEM),
-        scratch_shapes=[pltpu.VMEM(shape, a.dtype) for shape, a in zip(shapes, arrays)]
+        scratch_shapes=held
         + [
             pltpu.VMEM((slots, piece_rows, lanes), f32),
             pltpu.VMEM((slots, piece_rows, lanes), f32),
@@ -320,7 +323,7 @@
             pltpu.VMEM((inner, gathered, lanes), jnp.bfloat16),
             pltpu.VMEM((ex_count, examples, queries), f32),
             pltpu.VMEM((ex_count, examples, queries), f32),
-            pltpu.SemaphoreType.DMA((len(arrays),)),
+            pltpu.SemaphoreType.DMA((5 + 2 * examples,)),
             pltpu.SemaphoreType.DMA((slots,)),
             pltpu.SemaphoreType.DMA((slots,)),
             pltpu.SemaphoreType.DMA((outer,)),

time: 23.3 us -> 21.8 us (0.936)
  Pallas kernels: 21.8 us -> 20.9 us
  local copies, waits for them, and re-layouts: 1.24 us -> 0.56 us
    pallas_call x1, Pallas kernels: 21.8 us -> 20.9 us  [per_device(): pl.pallas_call(functools.partial(body, seq_count, ex_count, inner), out_s...]
    unnamed x1, local copies, waits for them, and re-layouts: 1.24 us -> 0.56 us
where the time goes in v2:
time: 21.8 us; the launch traced here: 21.5 us
  Pallas kernels  20.9 us (96%)
  local copies, waits for them, and re-layouts  0.56 us (3%)
    pallas_call x1, Pallas kernels, per_device(): pl.pallas_call(functools.partial(body, seq_count, ex_count, inner), out_s...  20.9 us
    unnamed x1, local copies, waits for them, and re-layouts  0.56 us

profile of v2, /device:TPU:0, one launch (start us, length us, event | category | flops | bytes accessed | tf_op | source)
XLA Modules:
  0.0 21.5 jit_solution(7284758617706680477)
XLA Ops:
  0.0 20.9 %scores.1 = f32[2,128]{1,0:T(2,128)S(1)} custom-call(s32[2]{0:T(128)} %lengths_ref.1, s32[32]{0:T(128)} %in_blocks_ref.1, s32[40]{0:T(128)} %out_blocks_ref.1, bf16[2,128,4096]{2,1,0:T(8,128)(2,1)} %acts_hbm.1, bf16[2,128,5120]{2,1,0:T(8,128)(2,1)} %grads_hbm.1, bf16[32,128,128]{2,1,0:T(8,128)(2,1)} %in_tiles_hbm.1, s32[32,128]{1,0:T(8,128)} %in_signs_hbm.1, ...), custom_call_target="tpu_custom_call" | custom-call | tf_op jit(solution)/shard_map/scores/pallas_call | solution.py:310
  21.0 0.6 %copy.12 = f32[2,128]{1,0:T(2,128)} copy(f32[2,128]{1,0:T(2,128)S(1)} %scores.1) | data formatting | bytes 2048
